TPU v7x, 1024 devices: a whole 8x8x8 slice. The times are simulated.
1024 devices in a mesh: rep: 8 (over x_lo, core), col: 128 (over x_hi, y, z).
Axes of the slice: x: 8 (x_hi: 2, x_lo: 4; x = x_hi * 4 + x_lo), y: 8, z: 8, core: 2. Of those that a mesh axis runs over, the one named last changes fastest.
Arguments:
- tokens_learn: bfloat16 [5120, 2048], P(None, 'rep'), may hold values from -6 to 6
- cotangent: bfloat16 [2048, 27648], P('rep', 'col'), may hold values from -6 to 6
- sample_ids: int32 [8, 256], P('rep'), may hold values from 0 to 7, never falling along the last dimension, each value on 1 to 64 neighbouring positions
- advantage: float32 [8, 8], P('rep'), may hold values from -2 to 2
- up_weight: bfloat16 [5120, 27648], P('rep', 'col'), may hold values from -0.078125 to 0.078125
- first_moment: float32 [5120, 27648], P('rep', 'col'), may hold values from -3 to 3
- second_moment: float32 [5120, 27648], P('rep', 'col'), may hold values from 0.05 to 1
- rollout_rows: bfloat16 [1024, 5120], P('rep', 'col'), may hold values from -6 to 6
- down_proj: bfloat16 [5120, 27648], P(None, 'col'), may hold values from -0.0390625 to 0.0390625
- live_lengths: int32 [8, 4], P('rep'), may hold values from 1 to 32, 96 in all within a row
Outputs:
- new_weight: bfloat16 [5120, 27648], P('rep', 'col')
- new_first: float32 [5120, 27648], P('rep', 'col')
- new_second: float32 [5120, 27648], P('rep', 'col')
- rollout_out: bfloat16 [5120, 1024], P('col', 'rep')
Inputs may be any that keep to these rules, and one draw needn't show every extreme that they name: `sample_ids`: each lane's sample ids never fall along the lane, and each of the 8 samples has 1 to 64 tokens of that lane. `live_lengths`: the 4 lengths of a replica sum to 96, and one of them is 32.
All inputs are finite; a program needn't handle non-finite values.
Results may differ from a plain program's by a relative error of at most 0.019.
Values may be sent and summed in bfloat16 or wider, within the bound.
A program may use at most 64 MiB of HBM per device.

v0:
```python
import math

import jax
import jax.numpy as jnp
from jax import lax
from jax.sharding import Mesh
from jax.sharding import PartitionSpec as P

SEQS = 4
REP = ("rep_0", "rep_1")
COL = ("col_0", "col_1", "col_2")


first_decay = 0.9
second_decay = 0.95
learn_rate = 0.003
decay_weight = 0.1
adam_epsilon = 1e-08
first_bias = 1.0 - math.exp(100.0 * math.log(0.9))
second_bias = 1.0 - math.exp(100.0 * math.log(0.95))


def sum_in_order(pieces, axes, order):
    lengths = [lax.axis_size(a) for a in axes]
    pieces = pieces.reshape(*lengths, *pieces.shape[1:])
    pieces = pieces.transpose(*order, *range(len(axes), pieces.ndim))
    pieces = pieces.reshape(-1, *pieces.shape[len(axes) :])
    for k in order:
        pieces = lax.psum_scatter(pieces, axes[k], scatter_dimension=0, tiled=True)
    return pieces[0]


def in_blocks(shard, dim, devices):
    lengths = shard.shape
    pieces = shard.reshape(*lengths[:dim], devices, lengths[dim] // devices, *lengths[dim + 1 :])
    return jnp.moveaxis(pieces, dim, 0)


def summed_rows(shard, axes, order, dim):
    devices = lax.axis_size(axes)
    return sum_in_order(in_blocks(shard, dim, devices), axes, order)


def joined_along(pieces, dim):
    lengths = list(pieces.shape[1:])
    lengths[dim] *= pieces.shape[0]
    return jnp.moveaxis(pieces, 0, dim).reshape(lengths)


def all_blocks(shard, axes, order):
    pieces = shard[None]
    for k in order:
        pieces = lax.all_gather(pieces, axes[k], axis=0, tiled=True)
    held = [lax.axis_size(axes[k]) for k in reversed(order)]
    pieces = pieces.reshape(*held, *shard.shape)
    turned = sorted(range(len(order)), key=lambda place: order[len(order) - 1 - place])
    return pieces.transpose(*turned, *range(len(order), pieces.ndim)).reshape(-1, *shard.shape)


def gather_axes(shard, axes, order, dim):
    return joined_along(all_blocks(shard, axes, order), dim)


def turned_blocks(pieces, axes, order):
    inside = pieces.shape[1:]
    filled = pieces.reshape(*(lax.axis_size(a) for a in axes), *inside)
    for k in order:
        filled = lax.all_to_all(filled, axes[k], k, k, tiled=True)
    return filled.reshape(-1, *inside)


def core_and_chips(shard, groups, order, split_dim, concat_dim):
    devices = lax.axis_size(groups[0]) * lax.axis_size(groups[1])
    pieces = in_blocks(shard, split_dim, devices)
    return joined_along(turned_blocks(pieces, groups, order), concat_dim)


def token_scales(sample_ids, advantage):
    members = (sample_ids[..., :, None] == jnp.arange(advantage.shape[-1], dtype=jnp.int32)).astype(
        jnp.float32
    )
    counts = jnp.sum(members, axis=-2)
    ratios = advantage / counts
    return jnp.sum(members * ratios[..., None, :], axis=-1)


def adam_update(gradient, up_weight, first_moment, second_moment):
    new_first = first_decay * first_moment + (1.0 - first_decay) * gradient
    new_second = second_decay * second_moment + (1.0 - second_decay) * gradient * gradient
    direction = new_first / first_bias / (jnp.sqrt(new_second / second_bias) + adam_epsilon)
    weight_wide = up_weight.astype(jnp.float32)
    new_weight = (weight_wide - learn_rate * (direction + decay_weight * weight_wide)).astype(
        jnp.bfloat16
    )
    return (new_weight, new_first, new_second)


def live_rows(live_lengths, rows_each):
    slot_len = rows_each // SEQS
    positions = jnp.arange(rows_each, dtype=jnp.int32)
    which = positions // slot_len
    within = positions % slot_len
    picks = (which[:, None] == jnp.arange(SEQS, dtype=jnp.int32)[None, :]).astype(jnp.int32)
    limits = jnp.sum(live_lengths[:, None, :] * picks[None, :, :], axis=-1)
    return (within[None, :] < limits).astype(jnp.float32).reshape(-1)


def body(
    tokens_learn,
    cotangent,
    sample_ids,
    advantage,
    up_weight,
    first_moment,
    second_moment,
    rollout_rows,
    down_proj,
    live_lengths,
):
    token_scale = token_scales(sample_ids, advantage)[0]
    scaled = (token_scale[:, None] * cotangent.astype(jnp.float32)).astype(jnp.bfloat16)
    gradient = summed_rows(
        jnp.dot(tokens_learn, scaled, preferred_element_type=jnp.float32).astype(jnp.bfloat16),
        REP,
        (1, 0),
        0,
    ).astype(jnp.float32)
    new_weight, new_first, new_second = adam_update(
        gradient, up_weight, first_moment, second_moment
    )
    whole_rows = gather_axes(rollout_rows, COL, (0, 1, 2), 1)
    row_count = whole_rows.shape[0]
    regrouped = core_and_chips(whole_rows, ("rep_0", "rep_1"), (1, 0), 1, 0)
    partial_value = jnp.dot(regrouped, new_weight, preferred_element_type=jnp.float32)
    pre_act = summed_rows(partial_value.astype(jnp.bfloat16), REP, (1, 0), 0).astype(jnp.float32)
    live_mask = live_rows(live_lengths, row_count)
    activation = (jax.nn.silu(pre_act) * live_mask[:, None]).astype(jnp.bfloat16)
    act_turned = jnp.transpose(activation)
    rollout_out = summed_rows(
        jnp.dot(down_proj, act_turned, preferred_element_type=jnp.float32), COL, (1, 2, 0), 0
    ).astype(jnp.bfloat16)
    return (new_weight, new_first, new_second, rollout_out)


def solution(mesh):
    torus = Mesh(mesh.devices.reshape(4, 2, 2, 8, 8), ("rep_0", "rep_1", "col_0", "col_1", "col_2"))
    in_specs = (
        P(None, REP),
        P(REP, COL),
        P(REP, None),
        P(REP, None),
        P(REP, COL),
        P(REP, COL),
        P(REP, COL),
        P(REP, COL),
        P(None, COL),
        P(REP, None),
    )
    out_specs = (P(REP, COL), P(REP, COL), P(REP, COL), P(COL, REP))
    return jax.shard_map(body, mesh=torus, in_specs=in_specs, out_specs=out_specs, check_vma=False)
```

profile of v0, /device:TPU:1, one launch (start us, length us, event | category | flops | bytes accessed | tf_op | source)
XLA Modules:
  0.0 358.8 jit_solution(9136654578278017048)
XLA Ops:
  8.0 0.0 copy-start
  8.0 0.0 reduce-scatter.16.cloned.1.call-start
  8.1 0.9 convert_reduce_fusion
  9.0 0.7 fusion.17
  9.7 0.8 select_reduce_fusion
  10.4 0.0 copy-done
  10.4 3.2 fusion
  13.7 6.2 %reshape_reshape.15 = bf16[4,2,640,216]{2,1,0,3:T(2,128)(2,1)} reshape(bf16[5120,216]{0,1:T(8,128)(2,1)} %fusion) | data formatting | bytes 4423680 | tf_op jit(solution)/shard_map/reshape;reshape | solution.py:25
  19.9 3.3 copy.49
  23.2 0.0 copy-start.3
  23.2 0.0 reduce-scatter.16.cloned.1.call-update
  23.2 0.0 all-gather.3.cloned.1.call-start
  23.3 0.6 copy-done.3
  23.9 7.8 %all-gather = bf16[256,40]{0,1:T(8,128)(2,1)S(1)} all-gather(bf16[128,40]{0,1:T(8,128)(2,1)S(1)} %copy-done.3), channel_id=2, replica_groups=mesh['rep_0'=4,'rep_1'=2,'col_0'=2,'col_1'=8,'col_2'=8] {'col_0'}, dimensions={0}, use_global_device_ids=true | all-gather | bytes 30720 | tf_op jit(solution)/shard_map/all_gather | solution.py:53
  31.6 22.7 %all_gather.10 = bf16[16,128,40]{1,2,0:T(8,128)(2,1)} all-gather(bf16[2,128,40]{1,2,0:T(8,128)(2,1)S(1)} %copy_bitcast_fusion), channel_id=1, replica_groups=mesh['rep_0'=4,'rep_1'=2,'col_0'=2,'col_1'=8,'col_2'=8] {'col_1'}, dimensions={0}, use_global_device_ids=true | all-gather | bytes 184320 | tf_op jit(solution)/shard_map/all_gather | solution.py:53
  54.4 0.0 all-gather.3.cloned.1.call-update
  54.4 0.0 reduce-scatter.24.cloned.1.call-start
  54.4 4.1 %reduce-scatter.16.cloned.1.call-done = bf16[4,640,216]{1,2,0:T(8,128)(2,1)} async-done(((bf16[8,640,216]{1,2,0:T(8,128)(2,1)}), bf16[4,640,216]{1,2,0:T(8,128)(2,1)}) %reduce-scatter.16.cloned.1.call-update) | async-done | bytes 1105936 | tf_op jit(solution)/shard_map/reduce_scatter | solution.py:29
  58.6 0.0 reduce-scatter.24.cloned.1.call-update
  58.6 54.1 %all-gather.3.cloned.1.call-done = bf16[128,128,40]{1,2,0:T(8,128)(2,1)} async-done(((bf16[16,128,40]{1,2,0:T(8,128)(2,1)}), bf16[128,128,40]{1,2,0:T(8,128)(2,1)}) %all-gather.3.cloned.1.call-update) | async-done | bytes 1310736 | tf_op jit(solution)/shard_map/all_gather | solution.py:53
  112.8 2.6 copy.51
  115.3 2.4 copy.52
  117.7 10.8 %all_to_all.10 = bf16[4,2,128,640]{3,2,0,1:T(8,128)(2,1)S(1)} all-to-all(bf16[4,2,128,640]{3,2,0,1:T(8,128)(2,1)} %copy.52), channel_id=1, replica_groups=mesh['rep_0'=4,'rep_1'=2,'col_0'=2,'col_1'=8,'col_2'=8] {'rep_1'}, dimensions={1} | all-to-all | bytes 2621440 | tf_op jit(solution)/shard_map/all_to_all | solution.py:68
  128.6 0.0 copy-start.2
  128.6 1.2 copy.53
  129.8 4.6 %all-to-all-start.1 = ((bf16[4,2,128,640]{3,2,1,0:T(8,128)(2,1)}), bf16[4,2,128,640]{3,2,1,0:T(8,128)(2,1)}, u32[]{:S(2)}, u32[]{:S(2)}) async-start(bf16[4,2,128,640]{3,2,1,0:T(8,128)(2,1)} %copy.53), calls=%async_computation.2 | async-start | bytes 2621440 | tf_op jit(solution)/shard_map/all_to_all | solution.py:68
  134.4 0.0 reduce-scatter.18.cloned.1.call-start
  134.4 0.0 reduce-scatter.24.cloned.1.call-done
  134.4 0.0 copy-done.2
  134.4 2.7 fusion.4
  137.1 0.0 copy-start.1
  137.1 28.3 %all-to-all-done.1 = bf16[4,2,128,640]{3,2,1,0:T(8,128)(2,1)} async-done(((bf16[4,2,128,640]{3,2,1,0:T(8,128)(2,1)}), bf16[4,2,128,640]{3,2,1,0:T(8,128)(2,1)}, u32[]{:S(2)}, u32[]{:S(2)}) %all-to-all-start.1) | async-done | bytes 1310752 | tf_op jit(solution)/shard_map/all_to_all | solution.py:68
  165.4 0.0 copy-done.1
  165.4 0.0 copy-start.4
  165.4 2.0 fusion.1
  167.3 0.3 reshape_reshape.18
  167.7 0.8 copy.54
  168.5 0.0 reduce-scatter.18.cloned.1.call-update
  168.5 0.0 reduce-scatter.26.cloned.1.call-start
  168.5 19.7 %reduce-scatter.18.cloned.1.call-done = bf16[4,128,216]{1,2,0:T(8,128)(2,1)} async-done(((bf16[8,128,216]{1,2,0:T(8,128)(2,1)}), bf16[4,128,216]{1,2,0:T(8,128)(2,1)}) %reduce-scatter.18.cloned.1.call-update) | async-done | bytes 221200 | tf_op jit(solution)/shard_map/reduce_scatter | solution.py:29
  188.3 0.0 reduce-scatter.26.cloned.1.call-update
  188.3 0.0 reduce-scatter.20.cloned.1.call-start
  188.4 0.0 copy-done.4
  188.4 0.1 select_reduce_fusion.1
  188.5 30.0 %reduce-scatter.26.cloned.1.call-done = bf16[1,128,216]{1,2,0:T(8,128)(2,1)} async-done(((bf16[4,128,216]{1,2,0:T(8,128)(2,1)}), bf16[1,128,216]{1,2,0:T(8,128)(2,1)}) %reduce-scatter.26.cloned.1.call-update) | async-done | bytes 55312
  218.5 3.7 %convolution_bitcast_fusion = f32[5120,128]{0,1:T(8,128)} fusion(bf16[5120,216]{0,1:T(8,128)(2,1)} %param.18, bf16[1,128,216]{1,2,0:T(8,128)(2,1)} %reduce-scatter.26.cloned.1.call-done, f32[128]{0:T(128)S(1)} %compare_convert_fusion), kind=kOutput, calls=%fused_computation.1 | convolution fusion | flops 283309056 | bytes 4889088 | tf_op jit(solution)/shard_map/dot_general | solution.py:140
  222.2 3.2 copy.55
  225.5 3.5 copy.56
  228.9 0.0 reduce-scatter.20.cloned.1.call-update
  229.0 0.0 reduce-scatter.22.cloned.1.call-start
  229.0 46.6 %reduce-scatter.20.cloned.1.call-done = f32[16,40,128]{2,1,0:T(8,128)} async-done(((f32[128,40,128]{2,1,0:T(8,128)}), f32[16,40,128]{2,1,0:T(8,128)}) %reduce-scatter.20.cloned.1.call-update) | async-done | bytes 327696 | tf_op jit(solution)/shard_map/reduce_scatter | solution.py:29
  275.6 0.0 reduce-scatter.22.cloned.1.call-update
  275.6 0.0 reduce-scatter.28.cloned.1.call-start
  275.7 47.2 %reduce-scatter.22.cloned.1.call-done = f32[2,40,128]{2,1,0:T(8,128)} async-done(((f32[16,40,128]{2,1,0:T(8,128)}), f32[2,40,128]{2,1,0:T(8,128)}) %reduce-scatter.22.cloned.1.call-update) | async-done | bytes 40976 | tf_op jit(solution)/shard_map/reduce_scatter | solution.py:29
  322.8 0.0 reduce-scatter.28.cloned.1.call-update
  322.9 27.3 %reduce-scatter.28.cloned.1.call-done = f32[1,40,128]{2,1,0:T(8,128)} async-done(((f32[2,40,128]{2,1,0:T(8,128)}), f32[1,40,128]{2,1,0:T(8,128)}) %reduce-scatter.28.cloned.1.call-update) | async-done | bytes 20496
  350.2 1.3 convert_bitcast_fusion
  (3 shorter events, 0.0 us)
Async XLA Ops:
  8.0 2.4 copy-start
  8.0 50.6 %reduce-scatter.16.cloned.1.call-start = ((), (), s32[]{:S(2)}) async-start(), calls=%async_computation.9 | async-start | bytes 3317760 | tf_op jit(solution)/shard_map/reduce_scatter | solution.py:29
  23.2 0.7 copy-start.3
  23.2 89.5 %all-gather.3.cloned.1.call-start = ((), (), s32[]{:S(2)}) async-start(), calls=%async_computation.10 | async-start | bytes 1474560 | tf_op jit(solution)/shard_map/all_gather | solution.py:53
  54.4 80.0 %reduce-scatter.24.cloned.1.call-start = ((), (), s32[]{:S(2)}) async-start(), calls=%async_computation.14 | async-start | bytes 1382400
  128.6 5.8 %copy-start.2 = (bf16[640,216]{0,1:T(8,128)(2,1)S(1)}, bf16[640,216]{0,1:T(8,128)(2,1)}, u32[]{:S(2)}) copy-start(bf16[640,216]{0,1:T(8,128)(2,1)} %param.14) | copy-start | bytes 829444
  129.8 35.6 %all-to-all-start.1 = ((bf16[4,2,128,640]{3,2,1,0:T(8,128)(2,1)}), bf16[4,2,128,640]{3,2,1,0:T(8,128)(2,1)}, u32[]{:S(2)}, u32[]{:S(2)}) async-start(bf16[4,2,128,640]{3,2,1,0:T(8,128)(2,1)} %copy.53), calls=%async_computation.2 | async-start | bytes 2621440 | tf_op jit(solution)/shard_map/all_to_all | solution.py:68
  134.4 53.9 %reduce-scatter.18.cloned.1.call-start = ((), (), s32[]{:S(2)}) async-start(), calls=%async_computation.11 | async-start | bytes 663552 | tf_op jit(solution)/shard_map/reduce_scatter | solution.py:29
  137.1 28.3 %copy-start.1 = (bf16[640,216]{0,1:T(8,128)(2,1)}, bf16[640,216]{0,1:T(8,128)(2,1)S(1)}, u32[]{:S(2)}) copy-start(bf16[640,216]{0,1:T(8,128)(2,1)S(1)} %get-tuple-element.4) | copy-start | bytes 829444
  165.4 23.0 %copy-start.4 = (s32[1,4]{1,0:T(1,128)S(1)}, s32[1,4]{1,0:T(1,128)}, u32[]{:S(2)}) copy-start(s32[1,4]{1,0:T(1,128)} %param.19) | copy-start | bytes 52
  168.5 50.0 %reduce-scatter.26.cloned.1.call-start = ((), (), s32[]{:S(2)}) async-start(), calls=%async_computation.15 | async-start | bytes 276480
  188.3 87.3 %reduce-scatter.20.cloned.1.call-start = ((), (), s32[]{:S(2)}) async-start(), calls=%async_computation.12 | async-start | bytes 2949120 | tf_op jit(solution)/shard_map/reduce_scatter | solution.py:29
  229.0 93.9 %reduce-scatter.22.cloned.1.call-start = ((), (), s32[]{:S(2)}) async-start(), calls=%async_computation.13 | async-start | bytes 368640 | tf_op jit(solution)/shard_map/reduce_scatter | solution.py:29
  275.6 74.6 %reduce-scatter.28.cloned.1.call-start = ((), (), s32[]{:S(2)}) async-start(), calls=%async_computation.16 | async-start | bytes 61440
Sparse Core Ops, SparseCore 0:
  23.3 35.1 reduce-scatter.15
  62.0 50.8 reduce-scatter.23
  168.6 19.6 reduce-scatter.17
  191.5 26.9 reduce-scatter.25
  323.0 27.1 reduce-scatter.27
Sparse Core Ops, SparseCore 1:
  54.5 58.2 all-gather.2
  229.0 46.5 reduce-scatter.19
  278.8 44.0 reduce-scatter.21
where the time goes:
time: 360 us; the launch traced here: 359 us
  waiting for transfers between devices  258 us (72%)
  blocking collectives  41.3 us (11%)
  local copies, waits for them, and re-layouts  24.2 us (7%)
  between operations  15.5 us (4%)
  matrix products  8.94 us (2%)
  other arithmetic  6.53 us (2%)
  starting transfers between devices  4.88 us (1%)
    reduce_scatter x4, waiting for transfers between devices, sum_in_order(): pieces = lax.psum_scatter(pieces, axes[k], scatter_dimension=0, tiled=True)  118 us
    unnamed x11, waiting for transfers between devices  57.5 us
    all_gather x1, waiting for transfers between devices, all_blocks(): pieces = lax.all_gather(pieces, axes[k], axis=0, tiled=True)  54.1 us
    all_gather x2, blocking collectives, all_blocks(): pieces = lax.all_gather(pieces, axes[k], axis=0, tiled=True)  30.5 us
    all_to_all x1, waiting for transfers between devices, turned_blocks(): filled = lax.all_to_all(filled, axes[k], k, k, tiled=True)  28.3 us
    all_to_all x1, blocking collectives, turned_blocks(): filled = lax.all_to_all(filled, axes[k], k, k, tiled=True)  10.8 us
    another operation x3, local copies, waits for them, and re-layouts, sum_in_order(): pieces = pieces.reshape(*lengths, *pieces.shape[1:])  7.36 us
  transfers between devices with their start and end apart: 9, of which 8 were waited for; matrix products, arithmetic and copies ran while one was open for 3% of the time, Pallas kernels for 0%

commit v1 on v0

v1 whole, which is shorter than its diff:
```python
import math

import jax
import jax.numpy as jnp
from jax import lax
from jax.experimental import pallas as pl
from jax.experimental.pallas import tpu as pltpu
from jax.sharding import Mesh
from jax.sharding import PartitionSpec as P

SEQS = 4
REP = ("rep_0", "rep_1")
COL = ("col_0", "col_1", "col_2")
Q, K, XH, Y, Z = "rep_0", "rep_1", "col_0", "col_1", "col_2"
MESH = pl.DeviceIdType.MESH
F32 = jnp.float32
BF16 = jnp.bfloat16

first_decay = 0.9
second_decay = 0.95
learn_rate = 0.003
decay_weight = 0.1
adam_epsilon = 1e-08
first_bias = 1.0 - math.exp(100.0 * math.log(0.9))
second_bias = 1.0 - math.exp(100.0 * math.log(0.95))

BLK = 640
COLS = 216
TOK = 256
ROWS = 128
FEAT = 40
HALF = 320
PIECES = ((0, 64), (64, 64), (128, 48), (176, 40))
RING = (4, 3, 5, 2, 6, 1, 7)

S_TOK, S_SC, S_R, S_L, S_X1 = 0, 4, 5, 21, 37
S_2A, S_2B, S_3A, S_3B, S_PRE = 39, 47, 55, 63, 71
S_1DA, S_1DB, S_2DA, S_2DB, S_XH = 79, 87, 95, 103, 111
N_SEM = 112
L_TOK, L_W, L_M, L_V, L_DN, L_OUT = 0, 4, 5, 6, 7, 8
N_LOCAL = 11


def adam_update(gradient, up_weight, first_moment, second_moment):
    new_first = first_decay * first_moment + (1.0 - first_decay) * gradient
    new_second = second_decay * second_moment + (1.0 - second_decay) * gradient * gradient
    direction = new_first / first_bias / (jnp.sqrt(new_second / second_bias) + adam_epsilon)
    weight_wide = up_weight.astype(F32)
    new_weight = (weight_wide - learn_rate * (direction + decay_weight * weight_wide)).astype(BF16)
    return (new_weight, new_first, new_second)


def kernel(
    tok, cot, ids, adv, lens, w_in, m_in, v_in, x_in, down,
    w_out, m_out, v_out, o_out,
    tok_a, tok_b, sc_o, sc_p, part, r_in, l_in, r_send, l_send,
    gath, p_send, p_recv,
    w_s, m_s, v_s, w_n, m_n, v_n, dn, dn_t, of,
    a_send, a_recv, b_send, b_recv, own_a, sum_a, sum_b,
    a2_send, a2_recv, b2_send, b2_recv, x_send, x_recv,
    send, recv, local,
):
    q, k = lax.axis_index(Q), lax.axis_index(K)
    xh, y, z = lax.axis_index(XH), lax.axis_index(Y), lax.axis_index(Z)
    r = 2 * q + k

    def remote(src, dst, at_send, at_recv, where):
        return pltpu.make_async_remote_copy(
            src_ref=src,
            dst_ref=dst,
            send_sem=send.at[at_send],
            recv_sem=recv.at[at_recv],
            device_id=where,
            device_id_type=MESH,
        )

    leaving = []

    def send_to(src, dst, at_send, at_recv, where):
        copy = remote(src, dst, at_send, at_recv, where)
        copy.start()
        leaving.append(copy.wait_send)

    def arrived(dst, at_recv):
        remote(dst, dst, 0, at_recv, {K: 1 - k}).wait_recv()

    def sent(src, at_send):
        remote(src, src, at_send, 0, {K: 1 - k}).wait_send()

    barrier = pltpu.get_barrier_semaphore()

    def greet(where):
        pl.semaphore_signal(barrier, inc=1, device_id=where, device_id_type=MESH)

    from_q, from_k, from_x = y // 2, y % 2, q // 2
    from_y = [4 * (q % 2) + 2 * k + j for j in range(2)]
    mine_from = [(from_q == q) & (from_k == k) & (from_x == xh) & (from_y[j] == y) for j in range(2)]
    to_q, to_k = 2 * xh + y // 4, (y // 2) % 2
    mine_to = [(to_q == q) & (to_k == k) & (xh == h) & (r == y) for h in range(2)]

    for d in range(1, 8):
        other = (r + d) % 8
        greet({Q: other // 2, K: other % 2})
        greet({Y: (y + d) % 8})
        greet({Z: (z + d) % 8})
    greet({XH: 1 - xh})
    for j in range(2):

        @pl.when(jnp.logical_not(mine_from[j]))
        def _():
            greet({Q: from_q, K: from_k, XH: from_x, Y: from_y[j], Z: z})

    def block_rows(b, parity):
        return pl.ds(pl.multiple_of((2 * b + parity) * BLK, BLK), BLK)

    order = (3, 0, 2, 1)
    loads = [pltpu.make_async_copy(tok.at[block_rows(b, k)], tok_a.at[b], local.at[L_TOK + b]) for b in range(4)]
    for b in order:
        loads[b].start()
    late = [
        pltpu.make_async_copy(w_in, w_s, local.at[L_W]),
        pltpu.make_async_copy(m_in, m_s, local.at[L_M]),
        pltpu.make_async_copy(v_in, v_s, local.at[L_V]),
        pltpu.make_async_copy(down, dn, local.at[L_DN]),
    ]
    for copy in late:
        copy.start()

    sample = lax.broadcasted_iota(jnp.int32, (8, TOK), 0)
    members = (ids[...] == sample).astype(F32)
    counts = jnp.sum(members, axis=1, keepdims=True)
    eye = lax.broadcasted_iota(jnp.int32, (8, 8), 0) == lax.broadcasted_iota(jnp.int32, (8, 8), 1)
    tall = jnp.sum(jnp.where(eye, adv[...], 0.0), axis=1, keepdims=True)
    scale = jnp.sum(members * (tall / counts), axis=0, keepdims=True)
    sc_o[...] = (scale * cot[...].astype(F32)).astype(BF16)

    pl.semaphore_wait(barrier, 24 - mine_to[0].astype(jnp.int32) - mine_to[1].astype(jnp.int32))

    for h in range(2):

        @pl.when(jnp.logical_not(mine_to[h]))
        def _():
            remote(x_in, gath.at[r, y % 2, z], S_X1 + h, S_X1 + y % 2, {Q: to_q, K: to_k, XH: h, Y: r, Z: z}).start()

        @pl.when(mine_to[h])
        def _():
            gath[r, y % 2, z] = x_in[...]

    send_to(sc_o, sc_p, S_SC, S_SC, {K: 1 - k})
    for b in order:
        send_to(tok.at[block_rows(b, 1 - k)], tok_b.at[b], S_TOK + b, S_TOK + b, {K: 1 - k})

    def running(b, s, first, sums, out, at, target):
        rows = pl.ds(*PIECES[s])
        value = part[b, rows]
        if not first:
            arrived(sums.at[b, rows], at + 4 * b + s)
            value = value + sums[b, rows].astype(F32)
        out[b, rows] = value.astype(BF16)
        remote(out.at[b, rows], sums.at[b, rows], at + 4 * b + s, at + 4 * b + s, {Q: target}).start()

    def right(b, s, first):
        running(b, s, first, r_in, r_send, S_R, q + 1)

    def left(b, s, first):
        running(b, s, first, l_in, l_send, S_L, q - 1)

    def over_tokens(scaled, tokens):
        return lax.dot_general(scaled, tokens, (((1,), (1,)), ((), ())), preferred_element_type=F32)

    arrived(sc_p, S_SC)
    for b in order:
        loads[b].wait()
        arrived(tok_b.at[b], S_TOK + b)

        part[b] = over_tokens(sc_o[...], tok_a[b]) + over_tokens(sc_p[...], tok_b[b])

        if b > 0:

            @pl.when(q == 0)
            def _():
                for s in range(4):
                    right(b, s, True)

        if b < 3:

            @pl.when(q == 3)
            def _():
                for s in range(4):
                    left(b, s, True)

    for j in range(2):

        @pl.when(jnp.logical_not(mine_from[j]))
        def _():
            arrived(gath.at[y, j, z], S_X1 + j)

    for d in RING:
        oz, oy = (z + d) % 8, (y + d) % 8
        here = gath.at[y, 0, z]
        send_to(here, here, S_2A + oz, S_2A + z, {Z: oz})
        here = gath.at[y, 1, z]
        send_to(here, here, S_2B + oy, S_2B + y, {Y: oy})

    @pl.when((q > 0) & (q < 3))
    def _():
        for s in range(4):
            right(3, s, False)
            left(0, s, False)

    for d in reversed(RING):
        oz = (z + d) % 8
        arrived(gath.at[y, 0, oz], S_2A + oz)
    for d in RING:
        oy = (y + d) % 8
        here = gath.at[y, 0]
        send_to(here, here, S_3A + oy, S_3A + y, {Y: oy})
    for d in reversed(RING):
        oy = (y + d) % 8
        arrived(gath.at[oy, 1, z], S_2B + oy)
    for d in RING:
        oz = (z + d) % 8
        here = gath.at[:, 1, z]
        send_to(here, here, S_3B + oz, S_3B + z, {Z: oz})

    @pl.when(q == 1)
    def _():
        for s in range(4):
            right(2, s, False)

    @pl.when(q == 2)
    def _():
        for s in range(4):
            left(1, s, False)

    late[3].wait()

    @pl.loop(0, 8)
    def _(i):
        at = pl.ds(pl.multiple_of(i * BLK, BLK), BLK)
        wide = jnp.concatenate([dn[:, at].astype(F32), jnp.zeros((256 - COLS, BLK), F32)], axis=0)
        dn_t[at] = jnp.transpose(wide)[:, :COLS].astype(BF16)

    @pl.when(q > 0)
    def _():
        for s in range(4):
            arrived(r_in.at[q, pl.ds(*PIECES[s])], S_R + 4 * q + s)

    @pl.when(q < 3)
    def _():
        for s in range(4):
            arrived(l_in.at[q, pl.ds(*PIECES[s])], S_L + 4 * q + s)

    for copy in late[:3]:
        copy.wait()
    has_left, has_right = q > 0, q < 3

    @pl.loop(0, 5)
    def _(i):
        lanes = pl.ds(pl.multiple_of(i * 128, 128), 128)
        for piece in PIECES:
            rows = pl.ds(*piece)
            gradient = part[q, rows, lanes]
            gradient = gradient + jnp.where(has_left, r_in[q, rows, lanes].astype(F32), 0.0)
            gradient = gradient + jnp.where(has_right, l_in[q, rows, lanes].astype(F32), 0.0)
            new = adam_update(gradient, w_s[rows, lanes], m_s[rows, lanes], v_s[rows, lanes])
            w_n[rows, lanes], m_n[rows, lanes], v_n[rows, lanes] = new

    outs = [
        pltpu.make_async_copy(w_n, w_out, local.at[L_OUT]),
        pltpu.make_async_copy(m_n, m_out, local.at[L_OUT + 1]),
        pltpu.make_async_copy(v_n, v_out, local.at[L_OUT + 2]),
    ]
    for copy in outs:
        copy.start()
        leaving.append(copy.wait)

    for d in RING:
        oy, oz = (y + d) % 8, (z + d) % 8
        arrived(gath.at[oy, 0], S_3A + oy)
        arrived(gath.at[:, 1, oz], S_3B + oz)

    def partial_of(other):
        return jnp.dot(w_n[...], gath[other].reshape(BLK, ROWS), preferred_element_type=F32)

    for d in (7, 6, 5, 4, 3, 2, 1):
        other = (r + d) % 8
        p_send[other] = partial_of(other).astype(BF16)
        send_to(p_send.at[other], p_recv.at[r], S_PRE + other, S_PRE + r, {Q: other // 2, K: other % 2})
    pre = partial_of(r)
    for d in range(1, 8):
        other = (r + d) % 8
        arrived(p_recv.at[other], S_PRE + other)
        pre = pre + p_recv[other].astype(F32)

    lane = lax.broadcasted_iota(jnp.int32, (1, ROWS), 1)
    slot_len = ROWS // SEQS
    limit = jnp.zeros((1, ROWS), jnp.int32)
    for s in range(SEQS):
        limit = jnp.where(lane // slot_len == s, lens[0, s], limit)
    live = lane % slot_len < limit
    act = jnp.where(live, pre / (1.0 + jnp.exp(-pre)), 0.0).astype(BF16)

    for n, d in enumerate(RING + (0,)):
        oy = (y + d) % 8
        rows = pl.ds(pl.multiple_of(oy * HALF, HALF), HALF)
        value = jnp.dot(dn_t[rows], act, preferred_element_type=F32)
        if d == 0:
            own_a[...] = value
        else:
            a_send[oy] = value.astype(BF16)
            send_to(a_send.at[oy], a_recv.at[y], S_1DA + oy, S_1DA + y, {Y: oy})
        of[pl.ds(n * HALF, HALF)] = jnp.dot(
            dn_t[pl.ds(8 * HALF + n * HALF, HALF)], act, preferred_element_type=F32
        )

    def turned(oz):
        return jnp.concatenate(
            [of[pl.ds(pl.multiple_of(i * HALF + oz * FEAT, 8), FEAT)] for i in range(8)], axis=0
        )

    for d in RING:
        oz = (z + d) % 8
        b_send[oz] = turned(oz).astype(BF16)
        send_to(b_send.at[oz], b_recv.at[z], S_1DB + oz, S_1DB + z, {Z: oz})

    value = own_a[...]
    for d in RING:
        oy = (y + d) % 8
        arrived(a_recv.at[oy], S_1DA + oy)
        value = value + a_recv[oy].astype(F32)
    sum_a[...] = value
    for d in RING:
        oz = (z + d) % 8
        a2_send[oz] = sum_a[pl.ds(pl.multiple_of(oz * FEAT, 8), FEAT)].astype(BF16)
        send_to(a2_send.at[oz], a2_recv.at[z], S_2DA + oz, S_2DA + z, {Z: oz})

    value = turned(z)
    for d in RING:
        oz = (z + d) % 8
        arrived(b_recv.at[oz], S_1DB + oz)
        value = value + b_recv[oz].astype(F32)
    sum_b[...] = value
    for d in RING:
        oy = (y + d) % 8
        b2_send[oy] = sum_b[pl.ds(pl.multiple_of(oy * FEAT, 8), FEAT)].astype(BF16)
        send_to(b2_send.at[oy], b2_recv.at[y], S_2DB + oy, S_2DB + y, {Y: oy})

    res_a = sum_a[pl.ds(pl.multiple_of(z * FEAT, 8), FEAT)]
    for d in RING:
        oz = (z + d) % 8
        arrived(a2_recv.at[oz], S_2DA + oz)
        res_a = res_a + a2_recv[oz].astype(F32)
    res_b = sum_b[pl.ds(pl.multiple_of(y * FEAT, 8), FEAT)]
    for d in RING:
        oy = (y + d) % 8
        arrived(b2_recv.at[oy], S_2DB + oy)
        res_b = res_b + b2_recv[oy].astype(F32)

    x_send[...] = jnp.where(xh == 0, res_b, res_a)
    send_to(x_send, x_recv, S_XH, S_XH, {XH: 1 - xh})
    arrived(x_recv, S_XH)
    o_out[...] = (jnp.where(xh == 0, res_a, res_b) + x_recv[...]).astype(BF16)

    for wait in leaving:
        wait()
    for b in range(4):
        for s in range(4):
            rows = pl.ds(*PIECES[s])

            @pl.when(q < b)
            def _():
                sent(r_send.at[b, rows], S_R + 4 * b + s)

            @pl.when(q > b)
            def _():
                sent(l_send.at[b, rows], S_L + 4 * b + s)

    for h in range(2):

        @pl.when(jnp.logical_not(mine_to[h]))
        def _():
            sent(x_in, S_X1 + h)


def hand_over(*refs):
    given, given_small, kept, kept_small, held, sems = refs[:3], refs[3], refs[4:7], refs[7], refs[8:11], refs[11]
    cuts = ((0, 112), (112, COLS - 112))
    into = [
        [pltpu.make_async_copy(a.at[pl.ds(*c)], h.at[pl.ds(*c)], sems.at[2 * i + n]) for n, c in enumerate(cuts)]
        for i, (a, h) in enumerate(zip(given, held))
    ]
    back = [
        [pltpu.make_async_copy(h.at[pl.ds(*c)], b.at[pl.ds(*c)], sems.at[6 + 2 * i + n]) for n, c in enumerate(cuts)]
        for i, (h, b) in enumerate(zip(held, kept))
    ]
    for copies in into:
        for copy in copies:
            copy.start()
    kept_small[...] = given_small[...]
    for i in range(3):
        for n in range(2):
            into[i][n].wait()
            back[i][n].start()
    for i in range(3):
        for n in range(2):
            back[i][n].wait()


def body(tok, cot, ids, adv, lens, up, first, second, rows, down):
    vmem, hbm, smem = (
        pl.BlockSpec(memory_space=pltpu.VMEM),
        pl.BlockSpec(memory_space=pl.ANY),
        pl.BlockSpec(memory_space=pltpu.SMEM),
    )

    def buf(*shape, dtype=BF16):
        return pltpu.VMEM(shape, dtype)

    out_shape = (
        jax.ShapeDtypeStruct((COLS, BLK), BF16),
        jax.ShapeDtypeStruct((COLS, BLK), F32),
        jax.ShapeDtypeStruct((COLS, BLK), F32),
        jax.ShapeDtypeStruct((FEAT, ROWS), BF16),
    )
    new_weight, new_first, new_second, out = pl.pallas_call(
        kernel,
        out_shape=out_shape,
        in_specs=[hbm, vmem, vmem, vmem, smem, hbm, hbm, hbm, vmem, hbm],
        out_specs=(hbm, hbm, hbm, vmem),
        scratch_shapes=[
            buf(4, BLK, TOK), buf(4, BLK, TOK), buf(COLS, TOK), buf(COLS, TOK),
            buf(4, COLS, BLK, dtype=F32),
            buf(4, COLS, BLK), buf(4, COLS, BLK), buf(4, COLS, BLK), buf(4, COLS, BLK),
            buf(8, 2, 8, FEAT, ROWS), buf(8, COLS, ROWS), buf(8, COLS, ROWS),
            buf(COLS, BLK), buf(COLS, BLK, dtype=F32), buf(COLS, BLK, dtype=F32),
            buf(COLS, BLK), buf(COLS, BLK, dtype=F32), buf(COLS, BLK, dtype=F32),
            buf(COLS, 8 * BLK), buf(8 * BLK, COLS), buf(8 * HALF, ROWS, dtype=F32),
            buf(8, HALF, ROWS), buf(8, HALF, ROWS), buf(8, HALF, ROWS), buf(8, HALF, ROWS),
            buf(HALF, ROWS, dtype=F32), buf(HALF, ROWS, dtype=F32), buf(HALF, ROWS, dtype=F32),
            buf(8, FEAT, ROWS), buf(8, FEAT, ROWS), buf(8, FEAT, ROWS), buf(8, FEAT, ROWS),
            buf(FEAT, ROWS, dtype=F32), buf(FEAT, ROWS, dtype=F32),
            pltpu.SemaphoreType.DMA((N_SEM,)), pltpu.SemaphoreType.DMA((N_SEM,)),
            pltpu.SemaphoreType.DMA((N_LOCAL,)),
        ],
        compiler_params=pltpu.CompilerParams(
            collective_id=0, has_side_effects=True, vmem_limit_bytes=56 * 1024 * 1024
        ),
        name="step",
    )(tok, cot.T, ids, adv, lens, up.T, first.T, second.T, rows.T, down.T)
    new_weight, new_first, new_second, out = pl.pallas_call(
        hand_over,
        out_shape=out_shape,
        in_specs=[hbm, hbm, hbm, vmem],
        out_specs=(hbm, hbm, hbm, vmem),
        scratch_shapes=[
            buf(COLS, BLK), buf(COLS, BLK, dtype=F32), buf(COLS, BLK, dtype=F32),
            pltpu.SemaphoreType.DMA((12,)),
        ],
        name="hand_over",
    )(new_weight, new_first, new_second, out)
    return (new_weight.T, new_first.T, new_second.T, out)


def solution(mesh):
    torus = Mesh(mesh.devices.reshape(4, 2, 2, 8, 8), (Q, K, XH, Y, Z))
    in_specs = (
        P(None, REP),
        P(REP, COL),
        P(REP, None),
        P(REP, None),
        P(REP, None),
        P(REP, COL),
        P(REP, COL),
        P(REP, COL),
        P(REP, COL),
        P(None, COL),
    )
    out_specs = (P(REP, COL), P(REP, COL), P(REP, COL), P(COL, REP))
    step = jax.shard_map(body, mesh=torus, in_specs=in_specs, out_specs=out_specs, check_vma=False)

    def run(tokens, cot, ids, adv, up, first, second, rows, down, lengths):
        return step(tokens, cot, ids, adv, lengths, up, first, second, rows, down)

    return run
```

time: 360 us -> 108 us (0.30)
  waiting for transfers between devices: 258 us -> 0 us
  Pallas kernels: 0 us -> 107 us
  blocking collectives: 41.3 us -> 0 us
  local copies, waits for them, and re-layouts: 24.2 us -> 0 us
  between operations: 15.5 us -> 0.64 us
  matrix products: 8.94 us -> 0 us
  other arithmetic: 6.53 us -> 0 us
  starting transfers between devices: 4.88 us -> 0 us
    reduce_scatter x4 -> x0, waiting for transfers between devices: 118 us -> none  [sum_in_order(): pieces = lax.psum_scatter(pieces, axes[k], scatter_dimension=0, tiled=True)]
    pallas_call x0 -> x2, Pallas kernels: none -> 107 us  [the longest x1 103 us: body(): pl.pallas_call(kernel, out_shape=out_shape, in_specs=[hbm, vmem, vmem, vm...]
    unnamed x11 -> x0, waiting for transfers between devices: 57.5 us -> none
    all_gather x1 -> x0, waiting for transfers between devices: 54.1 us -> none  [all_blocks(): pieces = lax.all_gather(pieces, axes[k], axis=0, tiled=True)]
    all_gather x2 -> x0, blocking collectives: 30.5 us -> none  [all_blocks(): pieces = lax.all_gather(pieces, axes[k], axis=0, tiled=True)]
    all_to_all x1 -> x0, waiting for transfers between devices: 28.3 us -> none  [turned_blocks(): filled = lax.all_to_all(filled, axes[k], k, k, tiled=True)]
    all_to_all x1 -> x0, blocking collectives: 10.8 us -> none  [turned_blocks(): filled = lax.all_to_all(filled, axes[k], k, k, tiled=True)]
    transpose x3 -> x0, local copies, waits for them, and re-layouts: 9.31 us -> none  [the longest x2 6.75 us: sum_in_order(): pieces = pieces.transpose(*order, *range(len(axes), pieces.ndim))]
  transfers between devices with their start and end apart: 9 -> 0, of which waited for: 8 -> 0; matrix products, arithmetic and copies ran while one was open for 3% -> 0% of each run, Pallas kernels for 0% -> 0%
where the time goes in v1:
time: 108 us; the launch traced here: 107 us
  Pallas kernels  107 us (99%)
    pallas_call x1, Pallas kernels, body(): pl.pallas_call(kernel, out_shape=out_shape, in_specs=[hbm, vmem, vmem, vm...  103 us
    pallas_call x1, Pallas kernels, body(): pl.pallas_call(hand_over, out_shape=out_shape, in_specs=[hbm, hbm, hbm, v...  3.49 us

profile of v1, /device:TPU:1, one launch (start us, length us, event | category | flops | bytes accessed | tf_op | source)
XLA Modules:
  0.0 107.2 jit_solution(18205372260074781442)
XLA Ops:
  0.6 103.1 %step.1 = (bf16[216,640]{1,0:T(8,128)(2,1)}, f32[216,640]{1,0:T(8,128)}, f32[216,640]{1,0:T(8,128)}, bf16[40,128]{1,0:T(8,128)(2,1)}) custom-call(bf16[5120,256]{1,0:T(8,128)(2,1)} %tok.1, bf16[216,256]{1,0:T(8,128)(2,1)} %bitcast.13, s32[1,256]{1,0:T(1,128)} %ids.1, f32[1,8]{1,0:T(1,128)} %adv.1, s32[1,4]{1,0:T(1,128)} %lens.1, bf16[216,640]{1,0:T(8,128)(2,1)} %bitcast.12, ...), custom_call_target="tpu_custom_call" | custom-call | tf_op jit(solution)/shard_map/step/pallas_call | solution.py:426
  103.7 3.5 %hand_over.1 = (bf16[216,640]{1,0:T(8,128)(2,1)}, f32[216,640]{1,0:T(8,128)}, f32[216,640]{1,0:T(8,128)}, bf16[40,128]{1,0:T(8,128)(2,1)}) custom-call(bf16[216,640]{1,0:T(8,128)(2,1)} %get-tuple-element.12.refs_0_, f32[216,640]{1,0:T(8,128)} %get-tuple-element.13.refs_1_, f32[216,640]{1,0:T(8,128)} %get-tuple-element.14.refs_2_, ...), custom_call_target="tpu_custom_call" | custom-call | tf_op jit(solution)/shard_map/hand_over/pallas_call | solution.py:451

commit v2 on v1

--- a/solution.py
+++ b/solution.py
@@ -55,8 +55,8 @@
     w_out, m_out, v_out, o_out,
     tok_a, tok_b, sc_o, sc_p, part, r_in, l_in, r_send, l_send,
     gath, p_send, p_recv,
-    w_s, m_s, v_s, w_n, m_n, v_n, dn, dn_t, of,
-    a_send, a_recv, b_send, b_recv, own_a, sum_a, sum_b,
+    w_s, m_s, v_s, w_n, m_n, v_n, dn, dn_y, dn_z,
+    a_send, a_recv, b_send, b_recv, sum_a, sum_b,
     a2_send, a2_recv, b2_send, b2_recv, x_send, x_recv,
     send, recv, local,
 ):
@@ -202,10 +202,14 @@
         here = gath.at[y, 1, z]
         send_to(here, here, S_2B + oy, S_2B + y, {Y: oy})
 
-    @pl.when((q > 0) & (q < 3))
+    @pl.when(q == 1)
     def _():
         for s in range(4):
             right(3, s, False)
+
+    @pl.when(q == 2)
+    def _():
+        for s in range(4):
             left(0, s, False)
 
     for d in reversed(RING):
@@ -226,20 +230,33 @@
     @pl.when(q == 1)
     def _():
         for s in range(4):
+            left(0, s, False)
+        for s in range(4):
             right(2, s, False)
 
     @pl.when(q == 2)
     def _():
         for s in range(4):
+            right(3, s, False)
+        for s in range(4):
             left(1, s, False)
 
     late[3].wait()
 
-    @pl.loop(0, 8)
+    def turned(at):
+        wide = jnp.concatenate([dn[:, at].astype(F32), jnp.zeros((256 - COLS, BLK), F32)], axis=0)
+        return jnp.transpose(wide)[:, :COLS]
+
+    @pl.loop(0, 4)
     def _(i):
-        at = pl.ds(pl.multiple_of(i * BLK, BLK), BLK)
-        wide = jnp.concatenate([dn[:, at].astype(F32), jnp.zeros((256 - COLS, BLK), F32)], axis=0)
-        dn_t[at] = jnp.transpose(wide)[:, :COLS].astype(BF16)
+        near = turned(pl.ds(pl.multiple_of(i * BLK, BLK), BLK)).astype(BF16)
+        dn_y[2 * i] = near[:HALF]
+        dn_y[2 * i + 1] = near[HALF:]
+        far = turned(pl.ds(pl.multiple_of((4 + i) * BLK, BLK), BLK))
+        for j in range(2):
+            for n in range(8):
+                at = j * HALF + n * FEAT
+                dn_z[n, 2 * i + j] = far[at : at + FEAT].astype(BF16)
 
     @pl.when(q > 0)
     def _():
@@ -301,30 +318,22 @@
     live = lane % slot_len < limit
     act = jnp.where(live, pre / (1.0 + jnp.exp(-pre)), 0.0).astype(BF16)
 
-    for n, d in enumerate(RING + (0,)):
-        oy = (y + d) % 8
-        rows = pl.ds(pl.multiple_of(oy * HALF, HALF), HALF)
-        value = jnp.dot(dn_t[rows], act, preferred_element_type=F32)
-        if d == 0:
-            own_a[...] = value
-        else:
-            a_send[oy] = value.astype(BF16)
-            send_to(a_send.at[oy], a_recv.at[y], S_1DA + oy, S_1DA + y, {Y: oy})
-        of[pl.ds(n * HALF, HALF)] = jnp.dot(
-            dn_t[pl.ds(8 * HALF + n * HALF, HALF)], act, preferred_element_type=F32
-        )
-
-    def turned(oz):
-        return jnp.concatenate(
-            [of[pl.ds(pl.multiple_of(i * HALF + oz * FEAT, 8), FEAT)] for i in range(8)], axis=0
-        )
-
-    for d in RING:
-        oz = (z + d) % 8
-        b_send[oz] = turned(oz).astype(BF16)
+    def down_y(oy):
+        return jnp.dot(dn_y[oy], act, preferred_element_type=F32)
+
+    def down_z(oz):
+        return jnp.dot(dn_z[oz].reshape(HALF, COLS), act, preferred_element_type=F32)
+
+    for d in RING:
+        oy, oz = (y + d) % 8, (z + d) % 8
+        a_send[oy] = down_y(oy).astype(BF16)
+        send_to(a_send.at[oy], a_recv.at[y], S_1DA + oy, S_1DA + y, {Y: oy})
+        b_send[oz] = down_z(oz).astype(BF16)
         send_to(b_send.at[oz], b_recv.at[z], S_1DB + oz, S_1DB + z, {Z: oz})
-
-    value = own_a[...]
+    sum_a[...] = down_y(y)
+    sum_b[...] = down_z(z)
+
+    value = sum_a[...]
     for d in RING:
         oy = (y + d) % 8
         arrived(a_recv.at[oy], S_1DA + oy)
@@ -335,7 +344,7 @@
         a2_send[oz] = sum_a[pl.ds(pl.multiple_of(oz * FEAT, 8), FEAT)].astype(BF16)
         send_to(a2_send.at[oz], a2_recv.at[z], S_2DA + oz, S_2DA + z, {Z: oz})
 
-    value = turned(z)
+    value = sum_b[...]
     for d in RING:
         oz = (z + d) % 8
         arrived(b_recv.at[oz], S_1DB + oz)
@@ -435,9 +444,9 @@
             buf(8, 2, 8, FEAT, ROWS), buf(8, COLS, ROWS), buf(8, COLS, ROWS),
             buf(COLS, BLK), buf(COLS, BLK, dtype=F32), buf(COLS, BLK, dtype=F32),
             buf(COLS, BLK), buf(COLS, BLK, dtype=F32), buf(COLS, BLK, dtype=F32),
-            buf(COLS, 8 * BLK), buf(8 * BLK, COLS), buf(8 * HALF, ROWS, dtype=F32),
+            buf(COLS, 8 * BLK), buf(8, HALF, COLS), buf(8, 8, FEAT, COLS),
             buf(8, HALF, ROWS), buf(8, HALF, ROWS), buf(8, HALF, ROWS), buf(8, HALF, ROWS),
-            buf(HALF, ROWS, dtype=F32), buf(HALF, ROWS, dtype=F32), buf(HALF, ROWS, dtype=F32),
+            buf(HALF, ROWS, dtype=F32), buf(HALF, ROWS, dtype=F32),
             buf(8, FEAT, ROWS), buf(8, FEAT, ROWS), buf(8, FEAT, ROWS), buf(8, FEAT, ROWS),
             buf(FEAT, ROWS, dtype=F32), buf(FEAT, ROWS, dtype=F32),
             pltpu.SemaphoreType.DMA((N_SEM,)), pltpu.SemaphoreType.DMA((N_SEM,)),

time: 108 us -> 94.4 us (0.87)
  Pallas kernels: 107 us -> 93.5 us
    pallas_call x1, Pallas kernels: 103 us -> 90 us  [body(): pl.pallas_call(kernel, out_shape=out_shape, in_specs=[hbm, vmem, vmem, vm...]
where the time goes in v2:
time: 94.4 us; the launch traced here: 94.1 us
  Pallas kernels  93.5 us (99%)
    pallas_call x1, Pallas kernels, body(): pl.pallas_call(kernel, out_shape=out_shape, in_specs=[hbm, vmem, vmem, vm...  90 us
    pallas_call x1, Pallas kernels, body(): pl.pallas_call(hand_over, out_shape=out_shape, in_specs=[hbm, hbm, hbm, v...  3.49 us

profile of v2, /device:TPU:1, one launch (start us, length us, event | category | flops | bytes accessed | tf_op | source)
XLA Modules:
  0.0 94.1 jit_solution(2351715875005394812)
XLA Ops:
  0.6 90.0 %step.1 = (bf16[216,640]{1,0:T(8,128)(2,1)}, f32[216,640]{1,0:T(8,128)}, f32[216,640]{1,0:T(8,128)}, bf16[40,128]{1,0:T(8,128)(2,1)}) custom-call(bf16[5120,256]{1,0:T(8,128)(2,1)} %tok.1, bf16[216,256]{1,0:T(8,128)(2,1)} %bitcast.13, s32[1,256]{1,0:T(1,128)} %ids.1, f32[1,8]{1,0:T(1,128)} %adv.1, s32[1,4]{1,0:T(1,128)} %lens.1, bf16[216,640]{1,0:T(8,128)(2,1)} %bitcast.12, ...), custom_call_target="tpu_custom_call" | custom-call | tf_op jit(solution)/shard_map/step/pallas_call | solution.py:435
  90.7 3.5 %hand_over.1 = (bf16[216,640]{1,0:T(8,128)(2,1)}, f32[216,640]{1,0:T(8,128)}, f32[216,640]{1,0:T(8,128)}, bf16[40,128]{1,0:T(8,128)(2,1)}) custom-call(bf16[216,640]{1,0:T(8,128)(2,1)} %get-tuple-element.12.refs_0_, f32[216,640]{1,0:T(8,128)} %get-tuple-element.13.refs_1_, f32[216,640]{1,0:T(8,128)} %get-tuple-element.14.refs_2_, ...), custom_call_target="tpu_custom_call" | custom-call | tf_op jit(solution)/shard_map/hand_over/pallas_call | solution.py:460

commit v3 on v2

--- a/solution.py
+++ b/solution.py
@@ -30,6 +30,9 @@
 ROWS = 128
 FEAT = 40
 HALF = 320
+LIVE = 96
+FOLD_COLS = 168
+FOLD_HALF = 240
 PIECES = ((0, 64), (64, 64), (128, 48), (176, 40))
 RING = (4, 3, 5, 2, 6, 1, 7)
 
@@ -50,11 +53,45 @@
     return (new_weight, new_first, new_second)
 
 
+def fold(value, rows):
+    quarter = value.shape[0] - rows
+    tail = value[rows:]
+    side = [pltpu.roll(tail, LIVE - 32 * s, 1) for s in range(3)]
+    if 3 * quarter < rows:
+        side.append(jnp.zeros((rows - 3 * quarter, ROWS), F32))
+    lane = lax.broadcasted_iota(jnp.int32, (rows, ROWS), 1)
+    return jnp.where(lane < LIVE, value[:rows], jnp.concatenate(side, axis=0))
+
+
+def unfold(value, length):
+    rows = value.shape[0]
+    quarter = length - rows
+    side = [pltpu.roll(value[s * quarter : (s + 1) * quarter], 32 + 32 * s, 1) for s in range(3)]
+    lane = lax.broadcasted_iota(jnp.int32, (quarter, ROWS), 1)
+    tail = jnp.where(lane < 32, side[0], jnp.where(lane < 64, side[1], side[2]))
+    whole = jnp.concatenate([value, tail], axis=0)
+    return jnp.where(lax.broadcasted_iota(jnp.int32, (length, ROWS), 1) < LIVE, whole, 0.0)
+
+
+def picks(lens, dim):
+    row = lax.broadcasted_iota(jnp.int32, (ROWS, ROWS), dim)
+    place = lax.broadcasted_iota(jnp.int32, (ROWS, ROWS), 1 - dim)
+    slot_len = ROWS // SEQS
+    slot, within = row // slot_len, row % slot_len
+    limit, ahead = jnp.zeros_like(row), jnp.zeros_like(row)
+    before = jnp.int32(0)
+    for s in range(SEQS):
+        limit = jnp.where(slot == s, lens[0, s], limit)
+        ahead = jnp.where(slot == s, before, ahead)
+        before = before + lens[0, s]
+    return jnp.where((within < limit) & (ahead + within == place), 1.0, 0.0).astype(BF16)
+
+
 def kernel(
     tok, cot, ids, adv, lens, w_in, m_in, v_in, x_in, down,
     w_out, m_out, v_out, o_out,
     tok_a, tok_b, sc_o, sc_p, part, r_in, l_in, r_send, l_send,
-    gath, p_send, p_recv,
+    x_live, gath, p_send, p_recv,
     w_s, m_s, v_s, w_n, m_n, v_n, dn, dn_y, dn_z,
     a_send, a_recv, b_send, b_recv, sum_a, sum_b,
     a2_send, a2_recv, b2_send, b2_recv, x_send, x_recv,
@@ -126,6 +163,8 @@
     for copy in late:
         copy.start()
 
+    x_live[...] = jnp.dot(x_in[...], picks(lens, 0), preferred_element_type=F32).astype(BF16)
+
     sample = lax.broadcasted_iota(jnp.int32, (8, TOK), 0)
     members = (ids[...] == sample).astype(F32)
     counts = jnp.sum(members, axis=1, keepdims=True)
@@ -140,11 +179,11 @@
 
         @pl.when(jnp.logical_not(mine_to[h]))
         def _():
-            remote(x_in, gath.at[r, y % 2, z], S_X1 + h, S_X1 + y % 2, {Q: to_q, K: to_k, XH: h, Y: r, Z: z}).start()
+            remote(x_live, gath.at[r, y % 2, z], S_X1 + h, S_X1 + y % 2, {Q: to_q, K: to_k, XH: h, Y: r, Z: z}).start()
 
         @pl.when(mine_to[h])
         def _():
-            gath[r, y % 2, z] = x_in[...]
+            gath[r, y % 2, z] = x_live[...]
 
     send_to(sc_o, sc_p, S_SC, S_SC, {K: 1 - k})
     for b in order:
@@ -298,7 +337,7 @@
         arrived(gath.at[:, 1, oz], S_3B + oz)
 
     def partial_of(other):
-        return jnp.dot(w_n[...], gath[other].reshape(BLK, ROWS), preferred_element_type=F32)
+        return fold(jnp.dot(w_n[...], gath[other].reshape(BLK, ROWS), preferred_element_type=F32), FOLD_COLS)
 
     for d in (7, 6, 5, 4, 3, 2, 1):
         other = (r + d) % 8
@@ -310,19 +349,14 @@
         arrived(p_recv.at[other], S_PRE + other)
         pre = pre + p_recv[other].astype(F32)
 
-    lane = lax.broadcasted_iota(jnp.int32, (1, ROWS), 1)
-    slot_len = ROWS // SEQS
-    limit = jnp.zeros((1, ROWS), jnp.int32)
-    for s in range(SEQS):
-        limit = jnp.where(lane // slot_len == s, lens[0, s], limit)
-    live = lane % slot_len < limit
-    act = jnp.where(live, pre / (1.0 + jnp.exp(-pre)), 0.0).astype(BF16)
+    pre = unfold(pre, COLS)
+    act = (pre / (1.0 + jnp.exp(-pre))).astype(BF16)
 
     def down_y(oy):
-        return jnp.dot(dn_y[oy], act, preferred_element_type=F32)
+        return fold(jnp.dot(dn_y[oy], act, preferred_element_type=F32), FOLD_HALF)
 
     def down_z(oz):
-        return jnp.dot(dn_z[oz].reshape(HALF, COLS), act, preferred_element_type=F32)
+        return fold(jnp.dot(dn_z[oz].reshape(HALF, COLS), act, preferred_element_type=F32), FOLD_HALF)
 
     for d in RING:
         oy, oz = (y + d) % 8, (z + d) % 8
@@ -330,26 +364,25 @@
         send_to(a_send.at[oy], a_recv.at[y], S_1DA + oy, S_1DA + y, {Y: oy})
         b_send[oz] = down_z(oz).astype(BF16)
         send_to(b_send.at[oz], b_recv.at[z], S_1DB + oz, S_1DB + z, {Z: oz})
-    sum_a[...] = down_y(y)
-    sum_b[...] = down_z(z)
-
-    value = sum_a[...]
+    own_a, own_b = down_y(y), down_z(z)
+
+    value = own_a
     for d in RING:
         oy = (y + d) % 8
         arrived(a_recv.at[oy], S_1DA + oy)
         value = value + a_recv[oy].astype(F32)
-    sum_a[...] = value
+    sum_a[...] = unfold(value, HALF)
     for d in RING:
         oz = (z + d) % 8
         a2_send[oz] = sum_a[pl.ds(pl.multiple_of(oz * FEAT, 8), FEAT)].astype(BF16)
         send_to(a2_send.at[oz], a2_recv.at[z], S_2DA + oz, S_2DA + z, {Z: oz})
 
-    value = sum_b[...]
+    value = own_b
     for d in RING:
         oz = (z + d) % 8
         arrived(b_recv.at[oz], S_1DB + oz)
         value = value + b_recv[oz].astype(F32)
-    sum_b[...] = value
+    sum_b[...] = unfold(value, HALF)
     for d in RING:
         oy = (y + d) % 8
         b2_send[oy] = sum_b[pl.ds(pl.multiple_of(oy * FEAT, 8), FEAT)].astype(BF16)
@@ -369,7 +402,8 @@
     x_send[...] = jnp.where(xh == 0, res_b, res_a)
     send_to(x_send, x_recv, S_XH, S_XH, {XH: 1 - xh})
     arrived(x_recv, S_XH)
-    o_out[...] = (jnp.where(xh == 0, res_a, res_b) + x_recv[...]).astype(BF16)
+    total = (jnp.where(xh == 0, res_a, res_b) + x_recv[...]).astype(BF16)
+    o_out[...] = jnp.dot(total, picks(lens, 1), preferred_element_type=F32).astype(BF16)
 
     for wait in leaving:
         wait()
@@ -389,7 +423,7 @@
 
         @pl.when(jnp.logical_not(mine_to[h]))
         def _():
-            sent(x_in, S_X1 + h)
+            sent(x_live, S_X1 + h)
 
 
 def hand_over(*refs):
@@ -441,11 +475,11 @@
             buf(4, BLK, TOK), buf(4, BLK, TOK), buf(COLS, TOK), buf(COLS, TOK),
             buf(4, COLS, BLK, dtype=F32),
             buf(4, COLS, BLK), buf(4, COLS, BLK), buf(4, COLS, BLK), buf(4, COLS, BLK),
-            buf(8, 2, 8, FEAT, ROWS), buf(8, COLS, ROWS), buf(8, COLS, ROWS),
+            buf(FEAT, ROWS), buf(8, 2, 8, FEAT, ROWS), buf(8, FOLD_COLS, ROWS), buf(8, FOLD_COLS, ROWS),
             buf(COLS, BLK), buf(COLS, BLK, dtype=F32), buf(COLS, BLK, dtype=F32),
             buf(COLS, BLK), buf(COLS, BLK, dtype=F32), buf(COLS, BLK, dtype=F32),
             buf(COLS, 8 * BLK), buf(8, HALF, COLS), buf(8, 8, FEAT, COLS),
-            buf(8, HALF, ROWS), buf(8, HALF, ROWS), buf(8, HALF, ROWS), buf(8, HALF, ROWS),
+            buf(8, FOLD_HALF, ROWS), buf(8, FOLD_HALF, ROWS), buf(8, FOLD_HALF, ROWS), buf(8, FOLD_HALF, ROWS),
             buf(HALF, ROWS, dtype=F32), buf(HALF, ROWS, dtype=F32),
             buf(8, FEAT, ROWS), buf(8, FEAT, ROWS), buf(8, FEAT, ROWS), buf(8, FEAT, ROWS),
             buf(FEAT, ROWS, dtype=F32), buf(FEAT, ROWS, dtype=F32),

time: 94.4 us -> 89.6 us (0.949)
  Pallas kernels: 93.5 us -> 88.7 us
    pallas_call x1, Pallas kernels: 90 us -> 85.2 us  [body(): pl.pallas_call(kernel, out_shape=out_shape, in_specs=[hbm, vmem, vmem, vm...]
where the time goes in v3:
time: 89.6 us; the launch traced here: 89.3 us
  Pallas kernels  88.7 us (99%)
    pallas_call x1, Pallas kernels, body(): pl.pallas_call(kernel, out_shape=out_shape, in_specs=[hbm, vmem, vmem, vm...  85.2 us
    pallas_call x1, Pallas kernels, body(): pl.pallas_call(hand_over, out_shape=out_shape, in_specs=[hbm, hbm, hbm, v...  3.49 us

profile of v3, /device:TPU:1, one launch (start us, length us, event | category | flops | bytes accessed | tf_op | source)
XLA Modules:
  0.0 89.3 jit_solution(15743577825008852665)
XLA Ops:
  0.6 85.2 %step.1 = (bf16[216,640]{1,0:T(8,128)(2,1)}, f32[216,640]{1,0:T(8,128)}, f32[216,640]{1,0:T(8,128)}, bf16[40,128]{1,0:T(8,128)(2,1)}) custom-call(bf16[5120,256]{1,0:T(8,128)(2,1)} %tok.1, bf16[216,256]{1,0:T(8,128)(2,1)} %bitcast.13, s32[1,256]{1,0:T(1,128)} %ids.1, f32[1,8]{1,0:T(1,128)} %adv.1, s32[1,4]{1,0:T(1,128)} %lens.1, bf16[216,640]{1,0:T(8,128)(2,1)} %bitcast.12, ...), custom_call_target="tpu_custom_call" | custom-call | tf_op jit(solution)/shard_map/step/pallas_call | solution.py:469
  85.8 3.5 %hand_over.1 = (bf16[216,640]{1,0:T(8,128)(2,1)}, f32[216,640]{1,0:T(8,128)}, f32[216,640]{1,0:T(8,128)}, bf16[40,128]{1,0:T(8,128)(2,1)}) custom-call(bf16[216,640]{1,0:T(8,128)(2,1)} %get-tuple-element.12.refs_0_, f32[216,640]{1,0:T(8,128)} %get-tuple-element.13.refs_1_, f32[216,640]{1,0:T(8,128)} %get-tuple-element.14.refs_2_, ...), custom_call_target="tpu_custom_call" | custom-call | tf_op jit(solution)/shard_map/hand_over/pallas_call | solution.py:494

commit v4 on v3

--- a/solution.py
+++ b/solution.py
@@ -207,8 +207,24 @@
     def over_tokens(scaled, tokens):
         return lax.dot_general(scaled, tokens, (((1,), (1,)), ((), ())), preferred_element_type=F32)
 
+    def spread_rows():
+        for j in range(2):
+
+            @pl.when(jnp.logical_not(mine_from[j]))
+            def _():
+                arrived(gath.at[y, j, z], S_X1 + j)
+
+        for d in RING:
+            oz, oy = (z + d) % 8, (y + d) % 8
+            here = gath.at[y, 0, z]
+            send_to(here, here, S_2A + oz, S_2A + z, {Z: oz})
+            here = gath.at[y, 1, z]
+            send_to(here, here, S_2B + oy, S_2B + y, {Y: oy})
+
     arrived(sc_p, S_SC)
     for b in order:
+        if b == order[-1]:
+            spread_rows()
         loads[b].wait()
         arrived(tok_b.at[b], S_TOK + b)
 
@@ -227,19 +243,6 @@
             def _():
                 for s in range(4):
                     left(b, s, True)
-
-    for j in range(2):
-
-        @pl.when(jnp.logical_not(mine_from[j]))
-        def _():
-            arrived(gath.at[y, j, z], S_X1 + j)
-
-    for d in RING:
-        oz, oy = (z + d) % 8, (y + d) % 8
-        here = gath.at[y, 0, z]
-        send_to(here, here, S_2A + oz, S_2A + z, {Z: oz})
-        here = gath.at[y, 1, z]
-        send_to(here, here, S_2B + oy, S_2B + y, {Y: oy})
 
     @pl.when(q == 1)
     def _():
@@ -339,10 +342,12 @@
     def partial_of(other):
         return fold(jnp.dot(w_n[...], gath[other].reshape(BLK, ROWS), preferred_element_type=F32), FOLD_COLS)
 
-    for d in (7, 6, 5, 4, 3, 2, 1):
-        other = (r + d) % 8
+    across = [(3 - q, k), (3 - q, 1 - k), ((q + 2) % 4, k), ((q + 2) % 4, 1 - k)]
+    beside = q + 1 - 2 * (q % 2)
+    for oq, ok in across + [(beside, k), (beside, 1 - k), (q, 1 - k)]:
+        other = 2 * oq + ok
         p_send[other] = partial_of(other).astype(BF16)
-        send_to(p_send.at[other], p_recv.at[r], S_PRE + other, S_PRE + r, {Q: other // 2, K: other % 2})
+        send_to(p_send.at[other], p_recv.at[r], S_PRE + other, S_PRE + r, {Q: oq, K: ok})
     pre = partial_of(r)
     for d in range(1, 8):
         other = (r + d) % 8
@@ -399,10 +404,10 @@
         arrived(b2_recv.at[oy], S_2DB + oy)
         res_b = res_b + b2_recv[oy].astype(F32)
 
-    x_send[...] = jnp.where(xh == 0, res_b, res_a)
+    x_send[...] = jnp.where(xh == 0, res_b, res_a).astype(BF16)
     send_to(x_send, x_recv, S_XH, S_XH, {XH: 1 - xh})
     arrived(x_recv, S_XH)
-    total = (jnp.where(xh == 0, res_a, res_b) + x_recv[...]).astype(BF16)
+    total = (jnp.where(xh == 0, res_a, res_b) + x_recv[...].astype(F32)).astype(BF16)
     o_out[...] = jnp.dot(total, picks(lens, 1), preferred_element_type=F32).astype(BF16)
 
     for wait in leaving:
@@ -427,27 +432,20 @@
 
 
 def hand_over(*refs):
-    given, given_small, kept, kept_small, held, sems = refs[:3], refs[3], refs[4:7], refs[7], refs[8:11], refs[11]
-    cuts = ((0, 112), (112, COLS - 112))
-    into = [
-        [pltpu.make_async_copy(a.at[pl.ds(*c)], h.at[pl.ds(*c)], sems.at[2 * i + n]) for n, c in enumerate(cuts)]
-        for i, (a, h) in enumerate(zip(given, held))
-    ]
-    back = [
-        [pltpu.make_async_copy(h.at[pl.ds(*c)], b.at[pl.ds(*c)], sems.at[6 + 2 * i + n]) for n, c in enumerate(cuts)]
-        for i, (h, b) in enumerate(zip(held, kept))
-    ]
-    for copies in into:
-        for copy in copies:
-            copy.start()
-    kept_small[...] = given_small[...]
-    for i in range(3):
-        for n in range(2):
-            into[i][n].wait()
-            back[i][n].start()
-    for i in range(3):
-        for n in range(2):
-            back[i][n].wait()
+    given, kept, held, sems = refs[:4], refs[4:8], refs[8:12], refs[12]
+    cuts = [(n, 0, 112) for n in range(3)] + [(n, 112, COLS - 112) for n in range(3)] + [(3, 0, FEAT)]
+    into, back = [], []
+    for i, (n, start, size) in enumerate(cuts):
+        rows = pl.ds(start, size)
+        into.append(pltpu.make_async_copy(given[n].at[rows], held[n].at[rows], sems.at[2 * i]))
+        back.append(pltpu.make_async_copy(held[n].at[rows], kept[n].at[rows], sems.at[2 * i + 1]))
+    for copy in into:
+        copy.start()
+    for first, second in zip(into, back):
+        first.wait()
+        second.start()
+    for copy in back:
+        copy.wait()
 
 
 def body(tok, cot, ids, adv, lens, up, first, second, rows, down):
@@ -482,7 +480,7 @@
             buf(8, FOLD_HALF, ROWS), buf(8, FOLD_HALF, ROWS), buf(8, FOLD_HALF, ROWS), buf(8, FOLD_HALF, ROWS),
             buf(HALF, ROWS, dtype=F32), buf(HALF, ROWS, dtype=F32),
             buf(8, FEAT, ROWS), buf(8, FEAT, ROWS), buf(8, FEAT, ROWS), buf(8, FEAT, ROWS),
-            buf(FEAT, ROWS, dtype=F32), buf(FEAT, ROWS, dtype=F32),
+            buf(FEAT, ROWS), buf(FEAT, ROWS),
             pltpu.SemaphoreType.DMA((N_SEM,)), pltpu.SemaphoreType.DMA((N_SEM,)),
             pltpu.SemaphoreType.DMA((N_LOCAL,)),
         ],
@@ -494,11 +492,11 @@
     new_weight, new_first, new_second, out = pl.pallas_call(
         hand_over,
         out_shape=out_shape,
-        in_specs=[hbm, hbm, hbm, vmem],
-        out_specs=(hbm, hbm, hbm, vmem),
+        in_specs=[hbm, hbm, hbm, hbm],
+        out_specs=(hbm, hbm, hbm, hbm),
         scratch_shapes=[
-            buf(COLS, BLK), buf(COLS, BLK, dtype=F32), buf(COLS, BLK, dtype=F32),
-            pltpu.SemaphoreType.DMA((12,)),
+            buf(COLS, BLK), buf(COLS, BLK, dtype=F32), buf(COLS, BLK, dtype=F32), buf(FEAT, ROWS),
+            pltpu.SemaphoreType.DMA((14,)),
         ],
         name="hand_over",
     )(new_weight, new_first, new_second, out)

time: 89.6 us -> 87.9 us (0.981)
  Pallas kernels: 88.7 us -> 86.9 us
    pallas_call x1, Pallas kernels: 3.49 us -> 2.19 us  [body(): pl.pallas_call(hand_over, out_shape=out_shape, in_specs=[hbm, hbm, hbm, h...]
where the time goes in v4:
time: 87.9 us; the launch traced here: 87.5 us
  Pallas kernels  86.9 us (99%)
    pallas_call x1, Pallas kernels, body(): pl.pallas_call(kernel, out_shape=out_shape, in_specs=[hbm, vmem, vmem, vm...  84.7 us
    pallas_call x1, Pallas kernels, body(): pl.pallas_call(hand_over, out_shape=out_shape, in_specs=[hbm, hbm, hbm, h...  2.19 us

profile of v4, /device:TPU:1, one launch (start us, length us, event | category | flops | bytes accessed | tf_op | source)
XLA Modules:
  0.0 87.5 jit_solution(11132696406891235299)
XLA Ops:
  0.6 84.7 %step.1 = (bf16[216,640]{1,0:T(8,128)(2,1)}, f32[216,640]{1,0:T(8,128)}, f32[216,640]{1,0:T(8,128)}, bf16[40,128]{1,0:T(8,128)(2,1)}) custom-call(bf16[5120,256]{1,0:T(8,128)(2,1)} %tok.1, bf16[216,256]{1,0:T(8,128)(2,1)} %bitcast.13, s32[1,256]{1,0:T(1,128)} %ids.1, f32[1,8]{1,0:T(1,128)} %adv.1, s32[1,4]{1,0:T(1,128)} %lens.1, bf16[216,640]{1,0:T(8,128)(2,1)} %bitcast.12, ...), custom_call_target="tpu_custom_call" | custom-call | tf_op jit(solution)/shard_map/step/pallas_call | solution.py:467
  85.3 2.2 %hand_over.1 = (bf16[216,640]{1,0:T(8,128)(2,1)}, f32[216,640]{1,0:T(8,128)}, f32[216,640]{1,0:T(8,128)}, bf16[40,128]{1,0:T(8,128)(2,1)}) custom-call(bf16[216,640]{1,0:T(8,128)(2,1)} %get-tuple-element.12.refs_0_, f32[216,640]{1,0:T(8,128)} %get-tuple-element.13.refs_1_, f32[216,640]{1,0:T(8,128)} %get-tuple-element.14.refs_2_, ...), custom_call_target="tpu_custom_call" | custom-call | tf_op jit(solution)/shard_map/hand_over/pallas_call | solution.py:492
